TPU v7x, 32 devices: a whole 2x2x4 slice. The times are simulated.
32 devices in a mesh: fsdp: 16 (over z, y, x), mp: 2 (over core).
Axes of the slice: x: 2, y: 2, z: 4, core: 2. Of those that a mesh axis runs over, the one named last changes fastest.
Arguments:
- values: bfloat16 [4096, 32], P('fsdp'), may hold values from -6 to 6
- lengths: int32 [64], P('fsdp'), may hold values from 1 to 64, 2560 in all
- w_in1: bfloat16 [64, 1280], P(None, 'fsdp'), may hold values from -0.75 to 0.75
- b_in1: bfloat16 [1280], P('fsdp'), may hold values from -3 to 3
- w_in2: bfloat16 [1280, 1280], P('fsdp'), may hold values from -0.15625 to 0.15625
- b_in2: bfloat16 [1280], P('fsdp'), may hold values from -3 to 3
- w_res: bfloat16 [64, 1280], P(None, 'fsdp'), may hold values from -0.75 to 0.75
- g_attn: bfloat16 [1280], P('fsdp'), may hold values from 0.099609375 to 1.8984375
- w_qkv: bfloat16 [1280, 3, 1280], P('fsdp', None, 'mp'), may hold values from -0.15625 to 0.15625
- w_out: bfloat16 [1280, 1280], P('mp', 'fsdp'), may hold values from -0.5 to 0.5
- g_mlp: bfloat16 [1280], P('fsdp'), may hold values from 0.099609375 to 1.8984375
- w_up: bfloat16 [1280, 1280], P('fsdp', 'mp'), may hold values from -0.15625 to 0.15625
- w_down: bfloat16 [1280, 1280], P('mp', 'fsdp'), may hold values from -0.25 to 0.25
- cotangent: bfloat16 [4096, 1280], P('fsdp'), may hold values from -6 to 6
Outputs:
- output: bfloat16 [4096, 1280], P('fsdp')
- d_values: float32 [4096, 32], P('fsdp')
- d_w_in1: float32 [64, 1280], P(None, 'fsdp')
- d_b_in1: float32 [1280], P('fsdp')
- d_w_in2: float32 [1280, 1280], P('fsdp')
- d_b_in2: float32 [1280], P('fsdp')
- d_w_res: float32 [64, 1280], P(None, 'fsdp')
- d_g_attn: float32 [1280], P('fsdp')
- d_w_qkv: float32 [1280, 3, 1280], P('fsdp', None, 'mp')
- d_w_out: float32 [1280, 1280], P('mp', 'fsdp')
- d_g_mlp: float32 [1280], P('fsdp')
- d_w_up: float32 [1280, 1280], P('fsdp', 'mp')
- d_w_down: float32 [1280, 1280], P('mp', 'fsdp')
Inputs may be any that keep to these rules, and one draw needn't show every extreme that they name: `lengths`: patches of series s; its padded slots come first.
All inputs are finite; a program needn't handle non-finite values. No bound on the sum of `lengths` on one device may be relied on, other than what follows from the above.
Results may differ from a plain program's by a relative error of at most 0.014.
Values may be sent and summed in bfloat16 or wider, within the bound.
A program may use at most 192 MiB of HBM per device.

v0:
```python
import jax
import jax.numpy as jnp
from jax import lax
from jax.sharding import PartitionSpec as P

HD = 80


def rotate(vectors, places):
    half_width = vectors.shape[-1] // 2
    frequency = 10000.0 ** (-2.0 * jnp.arange(half_width, dtype=jnp.float32) / vectors.shape[-1])
    angles = places[:, :, None, None] * frequency
    cosine = jnp.cos(angles)
    sine_val = jnp.sin(angles)
    first_half = vectors[..., :half_width]
    second_half = vectors[..., half_width:]
    return jnp.concatenate(
        [
            first_half * cosine - second_half * sine_val,
            second_half * cosine + first_half * sine_val,
        ],
        -1,
    )


def rms_norm(resid_rows, gain_vec):
    return (
        resid_rows
        * lax.rsqrt(jnp.mean(resid_rows * resid_rows, -1, keepdims=True) + 1e-06)
        * gain_vec
    )


def activate(up_rows):
    return jax.nn.gelu(up_rows, approximate=False)


def on_device(
    values,
    lengths,
    w_in1,
    b_in1,
    w_in2,
    b_in2,
    w_res,
    g_attn,
    w_qkv,
    w_out,
    g_mlp,
    w_up,
    w_down,
    cotangent,
):
    f32 = jnp.float32
    bf16 = jnp.bfloat16
    gathered = (
        lax.all_gather(w_in1, "fsdp", axis=1, tiled=True),
        lax.all_gather(b_in1, "fsdp", axis=0, tiled=True),
        lax.all_gather(w_in2, "fsdp", axis=0, tiled=True),
        lax.all_gather(b_in2, "fsdp", axis=0, tiled=True),
        lax.all_gather(w_res, "fsdp", axis=1, tiled=True),
        lax.all_gather(g_attn, "fsdp", axis=0, tiled=True),
        lax.all_gather(w_qkv, "fsdp", axis=0, tiled=True),
        lax.all_gather(w_out, "fsdp", axis=1, tiled=True),
        lax.all_gather(g_mlp, "fsdp", axis=0, tiled=True),
        lax.all_gather(w_up, "fsdp", axis=0, tiled=True),
        lax.all_gather(w_down, "fsdp", axis=1, tiled=True),
    )
    (
        full_in1,
        full_b1,
        full_in2,
        full_b2,
        full_res,
        full_gattn,
        full_qkv,
        full_out,
        full_gmlp,
        full_up,
        full_down,
    ) = gathered
    series = lengths.shape[0]
    seq_len = values.shape[0] // series
    patch_len = values.shape[1]
    slot_ids = jnp.arange(seq_len, dtype=jnp.int32)
    pad_count = seq_len - lengths
    padded = slot_ids[None, :] < pad_count[:, None]
    places = (slot_ids[None, :] - pad_count[:, None]).astype(f32)
    keep_mask = (1.0 - padded.astype(f32)).reshape(-1, 1)
    inputs = jnp.concatenate(
        [values.astype(f32) * keep_mask, jnp.broadcast_to(1.0 - keep_mask, values.shape)], 1
    ).astype(bf16)
    pre_act = jnp.dot(inputs, full_in1, preferred_element_type=f32) + full_b1.astype(f32)
    hidden = jax.nn.silu(pre_act).astype(bf16)
    resid0 = (
        jnp.dot(hidden, full_in2, preferred_element_type=f32)
        + full_b2.astype(f32)
        + jnp.dot(inputs, full_res, preferred_element_type=f32)
    )
    gain_attn = full_gattn.astype(f32)
    normed = rms_norm(resid0, gain_attn).astype(bf16)
    projected = jnp.einsum("td,dch->tch", normed, full_qkv, preferred_element_type=f32)
    local_heads = projected.shape[2] // HD
    head_shape = (series, seq_len, local_heads, HD)
    queries = rotate(projected[:, 0].reshape(head_shape), places).astype(bf16)
    key_rows = rotate(projected[:, 1].reshape(head_shape), places).astype(bf16)
    value_heads = projected[:, 2].reshape(head_shape).astype(bf16)
    causal = slot_ids[None, :] <= slot_ids[:, None]
    diagonal = slot_ids[None, :] == slot_ids[:, None]
    allowed = (causal[None] & (jnp.logical_not(padded)[:, None, :] | diagonal[None]))[:, None]
    scale = HD ** (-0.5)

    def score_block():
        raw = jnp.einsum("sqhe,skhe->shqk", queries, key_rows, preferred_element_type=f32) * scale
        return jnp.where(allowed, raw, -1e30)

    scores = score_block()
    row_max = jnp.max(scores, -1, keepdims=True)
    exponent = jnp.exp(scores - row_max)
    row_total = jnp.sum(exponent, -1, keepdims=True)
    log_total = row_max + jnp.log(row_total)
    attn_probs = (exponent / row_total).astype(bf16)
    attended = (
        jnp.einsum("shqk,skhe->sqhe", attn_probs, value_heads, preferred_element_type=f32)
        .reshape(-1, local_heads * HD)
        .astype(bf16)
    )
    branch_one = lax.psum(jnp.dot(attended, full_out, preferred_element_type=f32), "mp")
    resid1 = resid0 + branch_one
    gain_mlp = full_gmlp.astype(f32)
    normed2 = rms_norm(resid1, gain_mlp).astype(bf16)
    up_rows = jnp.dot(normed2, full_up, preferred_element_type=f32)
    mlp_hidden = activate(up_rows).astype(bf16)
    branch_two = lax.psum(
        jnp.dot(mlp_hidden, full_down, preferred_element_type=f32).astype(jnp.bfloat16), "mp"
    ).astype(jnp.float32)
    result = (resid1 + branch_two).astype(bf16)
    again = (
        lax.all_gather(w_in1, "fsdp", axis=1, tiled=True),
        lax.all_gather(b_in1, "fsdp", axis=0, tiled=True),
        lax.all_gather(w_in2, "fsdp", axis=0, tiled=True),
        lax.all_gather(b_in2, "fsdp", axis=0, tiled=True),
        lax.all_gather(w_res, "fsdp", axis=1, tiled=True),
        lax.all_gather(g_attn, "fsdp", axis=0, tiled=True),
        lax.all_gather(w_qkv, "fsdp", axis=0, tiled=True),
        lax.all_gather(w_out, "fsdp", axis=1, tiled=True),
        lax.all_gather(g_mlp, "fsdp", axis=0, tiled=True),
        lax.all_gather(w_up, "fsdp", axis=0, tiled=True),
        lax.all_gather(w_down, "fsdp", axis=1, tiled=True),
    )
    (
        back_in1,
        back_b1,
        back_in2,
        back_b2,
        back_res,
        back_gattn,
        back_qkv,
        back_out,
        back_gmlp,
        back_up,
        back_down,
    ) = again
    cot_rows = cotangent.astype(f32)
    grad_down = jnp.einsum("tf,td->fd", mlp_hidden, cotangent, preferred_element_type=f32)
    grad_hidden = jnp.einsum("td,fd->tf", cotangent, back_down, preferred_element_type=f32)
    unused_one, pull_mlp = jax.vjp(activate, up_rows)
    grad_up_rows = pull_mlp(grad_hidden)[0].astype(bf16)
    grad_up = jnp.einsum("td,tf->df", normed2, grad_up_rows, preferred_element_type=f32)
    norm_part2 = jnp.einsum("tf,df->td", grad_up_rows, back_up, preferred_element_type=f32)
    norm_grad2 = lax.psum(norm_part2, "mp")
    unused_two, pull_norm2 = jax.vjp(rms_norm, resid1, back_gmlp.astype(f32))
    resid_part1, grad_gmlp = pull_norm2(norm_grad2)
    resid1_grad = cot_rows + resid_part1
    out_grad = resid1_grad.astype(bf16)
    grad_out = jnp.einsum("th,td->hd", attended, out_grad, preferred_element_type=f32)
    attended_grad = (
        jnp.einsum("td,hd->th", out_grad, back_out, preferred_element_type=f32)
        .astype(bf16)
        .reshape(head_shape)
    )
    scores = score_block()
    probs_full = jnp.exp(scores - log_total)
    value_grad = jnp.einsum(
        "shqk,sqhe->skhe", probs_full.astype(bf16), attended_grad, preferred_element_type=f32
    )
    prob_grad = jnp.einsum(
        "sqhe,skhe->shqk", attended_grad, value_heads, preferred_element_type=f32
    )
    score_grad = (
        probs_full * (prob_grad - jnp.sum(prob_grad * probs_full, -1, keepdims=True))
    ).astype(bf16)
    query_grad = (
        jnp.einsum("shqk,skhe->sqhe", score_grad, key_rows, preferred_element_type=f32) * scale
    )
    key_grad = (
        jnp.einsum("shqk,sqhe->skhe", score_grad, queries, preferred_element_type=f32) * scale
    )
    width_local = local_heads * HD
    qkv_rows = jnp.stack(
        [
            rotate(query_grad, -places).reshape(-1, width_local),
            rotate(key_grad, -places).reshape(-1, width_local),
            value_grad.reshape(-1, width_local),
        ],
        1,
    ).astype(bf16)
    grad_qkv = jnp.einsum("td,tch->dch", normed, qkv_rows, preferred_element_type=f32)
    norm_part1 = jnp.einsum("tch,dch->td", qkv_rows, back_qkv, preferred_element_type=f32)
    norm_grad1 = lax.psum(norm_part1, "mp")
    unused_three, pull_norm1 = jax.vjp(rms_norm, resid0, back_gattn.astype(f32))
    resid_part0, grad_gattn = pull_norm1(norm_grad1)
    resid0_grad = (resid1_grad + resid_part0).astype(bf16)
    grad_in2 = jnp.einsum("th,td->hd", hidden, resid0_grad, preferred_element_type=f32)
    grad_b2 = jnp.sum(resid0_grad.astype(f32), 0)
    grad_res = jnp.einsum("tp,td->pd", inputs, resid0_grad, preferred_element_type=f32)
    hidden_grad = jnp.einsum("td,hd->th", resid0_grad, back_in2, preferred_element_type=f32)
    unused_four, pull_silu = jax.vjp(jax.nn.silu, pre_act)
    pre_grad = pull_silu(hidden_grad)[0].astype(bf16)
    grad_in1 = jnp.einsum("tp,th->ph", inputs, pre_grad, preferred_element_type=f32)
    grad_b1 = jnp.sum(pre_grad.astype(f32), 0)
    input_grad = jnp.einsum(
        "th,ph->tp", pre_grad, back_in1, preferred_element_type=f32
    ) + jnp.einsum("td,pd->tp", resid0_grad, back_res, preferred_element_type=f32)
    values_grad = input_grad[:, :patch_len] * keep_mask
    shares = tuple(
        (
            lax.psum_scatter(grad_in1, "fsdp", scatter_dimension=1, tiled=True),
            lax.psum_scatter(grad_b1, "fsdp", scatter_dimension=0, tiled=True),
            lax.psum_scatter(grad_in2, "fsdp", scatter_dimension=0, tiled=True),
            lax.psum_scatter(grad_b2, "fsdp", scatter_dimension=0, tiled=True),
            lax.psum_scatter(grad_res, "fsdp", scatter_dimension=1, tiled=True),
            lax.psum_scatter(grad_gattn, "fsdp", scatter_dimension=0, tiled=True),
            lax.psum_scatter(grad_qkv, "fsdp", scatter_dimension=0, tiled=True),
            lax.psum_scatter(grad_out, "fsdp", scatter_dimension=1, tiled=True),
            lax.psum_scatter(grad_gmlp, "fsdp", scatter_dimension=0, tiled=True),
            lax.psum_scatter(grad_up, "fsdp", scatter_dimension=0, tiled=True),
            lax.psum_scatter(grad_down, "fsdp", scatter_dimension=1, tiled=True),
        )
    )
    return (result, values_grad) + shares


def solution(mesh):
    in_specs = (
        P("fsdp", None),
        P("fsdp"),
        P(None, "fsdp"),
        P("fsdp"),
        P("fsdp", None),
        P("fsdp"),
        P(None, "fsdp"),
        P("fsdp"),
        P("fsdp", None, "mp"),
        P("mp", "fsdp"),
        P("fsdp"),
        P("fsdp", "mp"),
        P("mp", "fsdp"),
        P("fsdp", None),
    )
    out_specs = (
        P("fsdp", None),
        P("fsdp", None),
        P(None, "fsdp"),
        P("fsdp"),
        P("fsdp", None),
        P("fsdp"),
        P(None, "fsdp"),
        P("fsdp"),
        P("fsdp", None, "mp"),
        P("mp", "fsdp"),
        P("fsdp"),
        P("fsdp", "mp"),
        P("mp", "fsdp"),
    )
    return jax.shard_map(
        on_device, mesh=mesh, in_specs=in_specs, out_specs=out_specs, check_vma=False
    )
```

profile of v0, /device:TPU:10, one launch (start us, length us, event | category | flops | bytes accessed | tf_op | source)
XLA Modules:
  0.0 1254.7 jit_solution(667919393535561383)
XLA Ops:
  15.8 66.1 %all-reduce.9 = (bf16[1280]{0:T(1024)(128)(2,1)S(1)}, bf16[1280]{0:T(1024)(128)(2,1)S(1)}, bf16[1280]{0:T(1024)(128)(2,1)S(1)}, bf16[1280]{0:T(1024)(128)(2,1)}) all-reduce(bf16[1280]{0:T(1024)(128)(2,1)S(1)} %dynamic-update-slice.1, bf16[1280]{0:T(1024)(128)(2,1)S(1)} %dynamic-update-slice, ...), channel_id=1, replica_groups=mesh['fsdp'=16,'mp'=2] {'fsdp'}, use_global_device_ids=true, to_apply=%add.1 | all-reduce | flops 5120 | bytes 20480
  82.7 44.8 %all-gather = bf16[16,80,64]{1,2,0:T(8,128)(2,1)S(1)} all-gather(bf16[1,80,64]{1,2,0:T(8,128)(2,1)} %bitcast.81), channel_id=1, replica_groups=mesh['fsdp'=16,'mp'=2] {'fsdp'}, dimensions={0}, use_global_device_ids=true | all-gather | bytes 174080 | tf_op jit(solution)/shard_map/all_gather | solution.py:57
  127.9 38.5 %all-gather.1 = bf16[16,80,64]{1,2,0:T(8,128)(2,1)S(1)} all-gather(bf16[1,80,64]{1,2,0:T(8,128)(2,1)S(1)} %bitcast.82), channel_id=1, replica_groups=mesh['fsdp'=16,'mp'=2] {'fsdp'}, dimensions={0}, use_global_device_ids=true | all-gather | bytes 174080 | tf_op jit(solution)/shard_map/all_gather | solution.py:61
  175.0 4.0 fusion.35
  190.7 38.6 %all-gather.12.cloned.1.call-done = bf16[640,1280]{0,1:T(8,128)(2,1)} async-done(((bf16[640,80]{0,1:T(8,128)(2,1)}), bf16[640,1280]{0,1:T(8,128)(2,1)}) %all-gather.12.cloned.1.call-update) | async-done | bytes 1638416 | tf_op jit(solution)/shard_map/all_gather | solution.py:64
  234.0 18.6 %all-reduce.15.cloned.1.call-done = f32[256,1280]{1,0:T(8,128)} async-done(((f32[256,1280]{1,0:T(8,128)}), f32[256,1280]{1,0:T(8,128)}) %all-reduce.15.cloned.1.call-update) | async-done | bytes 1310736 | tf_op jit(solution)/shard_map/psum | solution.py:128
  254.1 59.7 %all-gather.14.cloned.1.call-done = bf16[1280,640]{1,0:T(8,128)(2,1)} async-done(((bf16[80,640]{1,0:T(8,128)(2,1)}), bf16[1280,640]{1,0:T(8,128)(2,1)}) %all-gather.14.cloned.1.call-update) | async-done | bytes 1638416 | tf_op jit(solution)/shard_map/all_gather | solution.py:66
  316.8 56.9 %all-gather.16.cloned.1.call-done = bf16[640,1280]{0,1:T(8,128)(2,1)} async-done(((bf16[640,80]{0,1:T(8,128)(2,1)}), bf16[640,1280]{0,1:T(8,128)(2,1)}) %all-gather.16.cloned.1.call-update) | async-done | bytes 1638416 | tf_op jit(solution)/shard_map/all_gather | solution.py:67
  373.7 4.7 add_convert_fusion.5
  384.8 16.1 %all-reduce.19.cloned.1.call-done = f32[256,1280]{1,0:T(8,128)} async-done(((f32[256,1280]{1,0:T(8,128)}), f32[256,1280]{1,0:T(8,128)}) %all-reduce.19.cloned.1.call-update) | async-done | bytes 1310736 | tf_op jit(solution)/shard_map/psum | solution.py:171
  402.5 21.4 %all-reduce.17.cloned.1.call-done = bf16[256,1280]{1,0:T(8,128)(2,1)} async-done(((bf16[256,1280]{1,0:T(8,128)(2,1)}), bf16[256,1280]{1,0:T(8,128)(2,1)}) %all-reduce.17.cloned.1.call-update) | async-done | bytes 655376 | tf_op jit(solution)/shard_map/psum | solution.py:134
  437.7 3.9 subtract_convert_fusion
  451.1 5.0 convolution_bitcast_fusion
  456.2 21.3 %all-reduce.21.cloned.1.call-done = f32[256,1280]{1,0:T(8,128)} async-done(((f32[256,1280]{1,0:T(8,128)}), f32[256,1280]{1,0:T(8,128)}) %all-reduce.21.cloned.1.call-update) | async-done | bytes 1310736 | tf_op jit(solution)/shard_map/psum | solution.py:210
  486.6 3.4 fusion.48
  499.8 4.0 fusion.50
  505.0 5.4 fusion.33
  511.2 65.2 %all-reduce.8 = (f32[1280]{0:T(1024)S(1)}, f32[1280]{0:T(1024)S(1)}, f32[1280]{0:T(1024)S(1)}, f32[1280]{0:T(1024)S(1)}) all-reduce(f32[1280]{0:T(1024)S(1)} %get-tuple-element.27, f32[1280]{0:T(1024)S(1)} %get-tuple-element.25, f32[1280]{0:T(1024)S(1)} %get-tuple-element.15, ...), channel_id=3, replica_groups=mesh['fsdp'=16,'mp'=2] {'fsdp'}, use_global_device_ids=true, to_apply=%region_13.14.clone | all-reduce | flops 5120 | bytes 40960
  581.5 46.6 %reduce-scatter.24.cloned.1.call-done = f32[80,64]{1,0:T(8,128)} async-done(((f32[1280,64]{1,0:T(8,128)}), f32[80,64]{1,0:T(8,128)}) %reduce-scatter.24.cloned.1.call-update) | async-done | bytes 20496
  629.6 86.2 %reduce-scatter.18.cloned.1.call-done = f32[80,640]{1,0:T(8,128)} async-done(((f32[1280,640]{1,0:T(8,128)}), f32[80,640]{1,0:T(8,128)}) %reduce-scatter.18.cloned.1.call-update) | async-done | bytes 204816 | tf_op jit(solution)/shard_map/reduce_scatter | solution.py:237
  715.9 85.1 %reduce-scatter.20.cloned.1.call-done = f32[640,80]{0,1:T(8,128)} async-done(((f32[640,1280]{0,1:T(8,128)}), f32[640,80]{0,1:T(8,128)}) %reduce-scatter.20.cloned.1.call-update) | async-done | bytes 204816 | tf_op jit(solution)/shard_map/reduce_scatter | solution.py:238
  800.9 84.7 %reduce-scatter.16.cloned.1.call-done = f32[640,80]{0,1:T(8,128)} async-done(((f32[640,1280]{0,1:T(8,128)}), f32[640,80]{0,1:T(8,128)}) %reduce-scatter.16.cloned.1.call-update) | async-done | bytes 204816 | tf_op jit(solution)/shard_map/reduce_scatter | solution.py:235
  885.6 150.4 %reduce-scatter.12.cloned.1.call-done = f32[80,1280]{1,0:T(8,128)} async-done(((f32[1280,1280]{1,0:T(8,128)}), f32[80,1280]{1,0:T(8,128)}) %reduce-scatter.12.cloned.1.call-update) | async-done | bytes 409616 | tf_op jit(solution)/shard_map/reduce_scatter | solution.py:230
  1036.0 212.2 %reduce-scatter.14.cloned.1.call-done = f32[80,3,640]{2,0,1:T(8,128)} async-done(((f32[1280,3,640]{2,0,1:T(8,128)}), f32[80,3,640]{2,0,1:T(8,128)}) %reduce-scatter.14.cloned.1.call-update) | async-done | bytes 614416 | tf_op jit(solution)/shard_map/reduce_scatter | solution.py:234
  (226 shorter events, 96.0 us)
Async XLA Ops:
  7.2 120.7 %copy-start.41 = (bf16[64,80]{1,0:T(8,128)(2,1)S(1)}, bf16[64,80]{1,0:T(8,128)(2,1)}, u32[]{:S(2)}) copy-start(bf16[64,80]{1,0:T(8,128)(2,1)} %param.20) | copy-start | bytes 30724
  7.2 162.6 %all-gather.8.cloned.1.call-start = ((), (), s32[]{:S(2)}) async-start(), calls=%async_computation.7 | async-start | bytes 3481600 | tf_op jit(solution)/shard_map/all_gather | solution.py:59
  7.9 166.5 %all-gather.10.cloned.1.call-start = ((), (), s32[]{:S(2)}) async-start(), calls=%async_computation.8 | async-start | bytes 5222400 | tf_op jit(solution)/shard_map/all_gather | solution.py:63
  8.7 220.7 %all-gather.12.cloned.1.call-start = ((), (), s32[]{:S(2)}) async-start(), calls=%async_computation.9 | async-start | bytes 1740800 | tf_op jit(solution)/shard_map/all_gather | solution.py:64
  9.4 243.2 %all-reduce.15.cloned.1.call-start = ((), (), s32[]{:S(2)}) async-start(), calls=%async_computation.10 | async-start | bytes 2621440 | tf_op jit(solution)/shard_map/psum | solution.py:128
  10.5 156.0 %copy-start.46 = (f32[256]{0:T(256)}, f32[256]{0:T(256)S(1)}, u32[]{:S(2)}) copy-start(f32[256]{0:T(256)S(1)} %sub.90) | copy-start | bytes 3076
  81.9 92.5 %copy-start.38 = (f32[1280]{0:T(1024)}, f32[1280]{0:T(1024)S(1)}, u32[]{:S(2)}) copy-start(f32[1280]{0:T(1024)S(1)} %convert_element_type.115) | copy-start | bytes 15364
  190.7 41.8 %copy-start.18 = (bf16[256,640]{1,0:T(8,128)(2,1)}, bf16[256,640]{1,0:T(8,128)(2,1)S(1)}, u32[]{:S(2)}) copy-start(bf16[256,640]{1,0:T(8,128)(2,1)S(1)} %convert_element_type.122) | copy-start | bytes 983044
  232.6 81.2 %all-gather.14.cloned.1.call-start = ((), (), s32[]{:S(2)}) async-start(), calls=%async_computation.11 | async-start | bytes 1740800 | tf_op jit(solution)/shard_map/all_gather | solution.py:66
  233.2 140.5 %all-gather.16.cloned.1.call-start = ((), (), s32[]{:S(2)}) async-start(), calls=%async_computation.12 | async-start | bytes 1740800 | tf_op jit(solution)/shard_map/all_gather | solution.py:67
  233.7 167.2 %all-reduce.19.cloned.1.call-start = ((), (), s32[]{:S(2)}) async-start(), calls=%async_computation.14 | async-start | bytes 2621440 | tf_op jit(solution)/shard_map/psum | solution.py:171
  380.9 43.1 %all-reduce.17.cloned.1.call-start = ((), (), s32[]{:S(2)}) async-start(), calls=%async_computation.13 | async-start | bytes 1310720 | tf_op jit(solution)/shard_map/psum | solution.py:134
  384.7 92.7 %all-reduce.21.cloned.1.call-start = ((), (), s32[]{:S(2)}) async-start(), calls=%async_computation.15 | async-start | bytes 2621440 | tf_op jit(solution)/shard_map/psum | solution.py:210
  456.2 123.9 %reduce-scatter.22.cloned.1.call-start = ((), (), s32[]{:S(2)}) async-start(), calls=%async_computation.21 | async-start | bytes 696320
  485.3 142.9 %reduce-scatter.24.cloned.1.call-start = ((), (), s32[]{:S(2)}) async-start(), calls=%async_computation.22 | async-start | bytes 696320
  486.6 229.3 %reduce-scatter.18.cloned.1.call-start = ((), (), s32[]{:S(2)}) async-start(), calls=%async_computation.19 | async-start | bytes 3481600 | tf_op jit(solution)/shard_map/reduce_scatter | solution.py:237
  490.1 310.8 %reduce-scatter.20.cloned.1.call-start = ((), (), s32[]{:S(2)}) async-start(), calls=%async_computation.20 | async-start | bytes 3481600 | tf_op jit(solution)/shard_map/reduce_scatter | solution.py:238
  493.7 391.9 %reduce-scatter.16.cloned.1.call-start = ((), (), s32[]{:S(2)}) async-start(), calls=%async_computation.18 | async-start | bytes 3481600 | tf_op jit(solution)/shard_map/reduce_scatter | solution.py:235
  498.5 537.5 %reduce-scatter.12.cloned.1.call-start = ((), (), s32[]{:S(2)}) async-start(), calls=%async_computation.16 | async-start | bytes 6963200 | tf_op jit(solution)/shard_map/reduce_scatter | solution.py:230
  503.8 744.4 %reduce-scatter.14.cloned.1.call-start = ((), (), s32[]{:S(2)}) async-start(), calls=%async_computation.17 | async-start | bytes 10444800 | tf_op jit(solution)/shard_map/reduce_scatter | solution.py:234
  510.4 68.3 %copy-start.30 = (bf16[1280,64]{0,1:T(8,128)(2,1)S(1)}, bf16[1280,64]{0,1:T(8,128)(2,1)}, u32[]{:S(2)}) copy-start(bf16[1280,64]{0,1:T(8,128)(2,1)} %copy-done.29) | copy-start | bytes 491524
  510.4 68.7 %copy-start.24 = (bf16[256,1280]{1,0:T(8,128)(2,1)S(1)}, bf16[256,1280]{1,0:T(8,128)(2,1)}, u32[]{:S(2)}) copy-start(bf16[256,1280]{1,0:T(8,128)(2,1)} %copy-done.23) | copy-start | bytes 1966084
  510.4 68.7 %copy-start.32 = (bf16[1280,64]{0,1:T(8,128)(2,1)S(1)}, bf16[1280,64]{0,1:T(8,128)(2,1)}, u32[]{:S(2)}) copy-start(bf16[1280,64]{0,1:T(8,128)(2,1)} %copy-done.31) | copy-start | bytes 491524
  510.4 69.0 %copy-start.47 = (f32[256]{0:T(256)S(1)}, f32[256]{0:T(256)}, u32[]{:S(2)}) copy-start(f32[256]{0:T(256)} %copy-done.46) | copy-start | bytes 3076
  (42 other events, 172.7 us)
Sparse Core Ops, SparseCore 0:
  10.8 70.6 all-gather.7
  84.1 85.1 all-gather.9
  172.0 57.2 all-gather.11
  232.7 19.8 all-reduce.14
  255.5 58.2 all-gather.13
  316.7 56.9 all-gather.15
  381.0 19.8 all-reduce.18
  403.8 20.1 all-reduce.16
  456.3 21.1 all-reduce.20
  485.4 67.0 reduce-scatter.21
  554.8 73.3 reduce-scatter.23
  630.9 84.9 reduce-scatter.17
  718.7 82.1 reduce-scatter.19
  803.7 81.8 reduce-scatter.15
  888.3 147.6 reduce-scatter.11
  1038.9 209.2 reduce-scatter.13
where the time goes:
time: 1260 us; the launch traced here: 1250 us
  waiting for transfers between devices  901 us (72%)
  blocking collectives  215 us (17%)
  matrix products  57.3 us (5%)
  local copies, waits for them, and re-layouts  43.2 us (3%)
  other arithmetic  21.6 us (2%)
  between operations  15.9 us (1%)
    reduce_scatter x1, waiting for transfers between devices, on_device(): lax.psum_scatter(grad_qkv, 'fsdp', scatter_dimension=0, tiled=True)  212 us
    reduce_scatter x1, waiting for transfers between devices, on_device(): lax.psum_scatter(grad_in2, 'fsdp', scatter_dimension=0, tiled=True)  150 us
    unnamed x2, blocking collectives  131 us
    reduce_scatter x1, waiting for transfers between devices, on_device(): lax.psum_scatter(grad_up, 'fsdp', scatter_dimension=0, tiled=True)  86.2 us
    reduce_scatter x1, waiting for transfers between devices, on_device(): lax.psum_scatter(grad_down, 'fsdp', scatter_dimension=1, tiled=True)  85.1 us
    reduce_scatter x1, waiting for transfers between devices, on_device(): lax.psum_scatter(grad_out, 'fsdp', scatter_dimension=1, tiled=True)  84.7 us
    all_gather x1, waiting for transfers between devices, on_device(): lax.all_gather(w_up, 'fsdp', axis=0, tiled=True)  59.7 us
    all_gather x1, waiting for transfers between devices, on_device(): lax.all_gather(w_down, 'fsdp', axis=1, tiled=True)  56.9 us
  transfers between devices with their start and end apart: 16, of which 13 were waited for; matrix products, arithmetic and copies ran while one was open for 5% of the time, Pallas kernels for 0%

commit v1 on v0

--- a/solution.py
+++ b/solution.py
@@ -4,6 +4,27 @@
 from jax.sharding import PartitionSpec as P
 
 HD = 80
+
+
+def collect(x, axis, dim):
+    size, index, width = (lax.axis_size(axis), lax.axis_index(axis), x.shape[dim])
+    right = [(i, (i + 1) % size) for i in range(size)]
+    downward = [(i, (i - 1) % size) for i in range(size)]
+    filled = jnp.zeros((*x.shape[:dim], size * width, *x.shape[dim + 1 :]), x.dtype)
+    filled = lax.dynamic_update_slice_in_dim(filled, x, index * width, axis=dim)
+    from_left = from_right = x
+    half = size // 2
+    for step in range(1, half + 1):
+        from_left = lax.ppermute(from_left, axis, right)
+        filled = lax.dynamic_update_slice_in_dim(
+            filled, from_left, (index - step) % size * width, axis=dim
+        )
+        if step < size - half:
+            from_right = lax.ppermute(from_right, axis, downward)
+            filled = lax.dynamic_update_slice_in_dim(
+                filled, from_right, (index + step) % size * width, axis=dim
+            )
+    return filled
 
 
 def rotate(vectors, places):
@@ -61,7 +82,7 @@
         lax.all_gather(w_res, "fsdp", axis=1, tiled=True),
         lax.all_gather(g_attn, "fsdp", axis=0, tiled=True),
         lax.all_gather(w_qkv, "fsdp", axis=0, tiled=True),
-        lax.all_gather(w_out, "fsdp", axis=1, tiled=True),
+        collect(w_out, "fsdp", 1),
         lax.all_gather(g_mlp, "fsdp", axis=0, tiled=True),
         lax.all_gather(w_up, "fsdp", axis=0, tiled=True),
         lax.all_gather(w_down, "fsdp", axis=1, tiled=True),

time: 1260 us -> 1340 us (1.063)
  waiting for transfers between devices: 901 us -> 956 us
  starting transfers between devices: 1.05 us -> 17.1 us
    ppermute x0 -> x15, waiting for transfers between devices: none -> 21.1 us  [the longest x8 21.1 us: collect(): from_left = lax.ppermute(from_left, axis, right)]
    all_gather x1, waiting for transfers between devices: 38.6 us -> 58 us  [on_device(): lax.all_gather(w_out, 'fsdp', axis=1, tiled=True)]
    psum x1, waiting for transfers between devices: 18.6 us -> 35.9 us  [on_device(): lax.psum(jnp.dot(attended, full_out, preferred_element_type=f32), 'mp')]
    ppermute x0 -> x15, starting transfers between devices: none -> 16 us  [the longest x7 14.2 us: collect(): from_right = lax.ppermute(from_right, axis, downward)]
  transfers between devices with their start and end apart: 16 -> 31, of which waited for: 13 -> 20; matrix products, arithmetic and copies ran while one was open for 5% -> 5% of each run, Pallas kernels for 0% -> 0%
where the time goes in v1:
time: 1340 us; the launch traced here: 1330 us
  waiting for transfers between devices  956 us (71%)
  blocking collectives  215 us (16%)
  matrix products  58.5 us (4%)
  local copies, waits for them, and re-layouts  53.1 us (4%)
  other arithmetic  18.2 us (1%)
  starting transfers between devices  17.1 us (1%)
  between operations  16.1 us (1%)
    reduce_scatter x1, waiting for transfers between devices, on_device(): lax.psum_scatter(grad_qkv, 'fsdp', scatter_dimension=0, tiled=True)  212 us
    reduce_scatter x1, waiting for transfers between devices, on_device(): lax.psum_scatter(grad_in2, 'fsdp', scatter_dimension=0, tiled=True)  151 us
    unnamed x2, blocking collectives  132 us
    reduce_scatter x1, waiting for transfers between devices, on_device(): lax.psum_scatter(grad_up, 'fsdp', scatter_dimension=0, tiled=True)  85.9 us
    reduce_scatter x1, waiting for transfers between devices, on_device(): lax.psum_scatter(grad_down, 'fsdp', scatter_dimension=1, tiled=True)  84.7 us
    reduce_scatter x1, waiting for transfers between devices, on_device(): lax.psum_scatter(grad_out, 'fsdp', scatter_dimension=1, tiled=True)  84.7 us
    all_gather x1, waiting for transfers between devices, on_device(): lax.all_gather(w_up, 'fsdp', axis=0, tiled=True)  59.7 us
    all_gather x1, waiting for transfers between devices, on_device(): lax.all_gather(w_out, 'fsdp', axis=1, tiled=True)  58 us
  transfers between devices with their start and end apart: 31, of which 20 were waited for; matrix products, arithmetic and copies ran while one was open for 5% of the time, Pallas kernels for 0%

profile of v1, /device:TPU:10, one launch (start us, length us, event | category | flops | bytes accessed | tf_op | source)
XLA Modules:
  0.0 1333.9 jit_solution(14566133085204311793)
XLA Ops:
  16.2 66.8 %all-reduce.9 = (bf16[1280]{0:T(1024)(128)(2,1)S(1)}, bf16[1280]{0:T(1024)(128)(2,1)S(1)}, bf16[1280]{0:T(1024)(128)(2,1)S(1)}, bf16[1280]{0:T(1024)(128)(2,1)}) all-reduce(bf16[1280]{0:T(1024)(128)(2,1)S(1)} %dynamic-update-slice.1, bf16[1280]{0:T(1024)(128)(2,1)S(1)} %dynamic-update-slice, ...), channel_id=1, replica_groups=mesh['fsdp'=16,'mp'=2] {'fsdp'}, use_global_device_ids=true, to_apply=%add.1 | all-reduce | flops 5120 | bytes 20480
  83.0 43.6 %all-gather = bf16[16,80,64]{1,2,0:T(8,128)(2,1)S(1)} all-gather(bf16[1,80,64]{1,2,0:T(8,128)(2,1)} %bitcast.81), channel_id=1, replica_groups=mesh['fsdp'=16,'mp'=2] {'fsdp'}, dimensions={0}, use_global_device_ids=true | all-gather | bytes 174080 | tf_op jit(solution)/shard_map/all_gather | solution.py:78
  127.3 39.6 %all-gather.1 = bf16[16,80,64]{1,2,0:T(8,128)(2,1)S(1)} all-gather(bf16[1,80,64]{1,2,0:T(8,128)(2,1)S(1)} %bitcast.82), channel_id=1, replica_groups=mesh['fsdp'=16,'mp'=2] {'fsdp'}, dimensions={0}, use_global_device_ids=true | all-gather | bytes 174080 | tf_op jit(solution)/shard_map/all_gather | solution.py:82
  182.8 3.9 collective-permute-done.4
  211.7 5.0 collective-permute-done.14
  221.0 4.0 fusion.35
  240.4 35.9 %all-reduce.15.cloned.1.call-done = f32[256,1280]{1,0:T(8,128)} async-done(((f32[256,1280]{1,0:T(8,128)}), f32[256,1280]{1,0:T(8,128)}) %all-reduce.15.cloned.1.call-update) | async-done | bytes 1310736 | tf_op jit(solution)/shard_map/psum | solution.py:149
  277.9 59.7 %all-gather.12.cloned.1.call-done = bf16[1280,640]{1,0:T(8,128)(2,1)} async-done(((bf16[80,640]{1,0:T(8,128)(2,1)}), bf16[1280,640]{1,0:T(8,128)(2,1)}) %all-gather.12.cloned.1.call-update) | async-done | bytes 1638416 | tf_op jit(solution)/shard_map/all_gather | solution.py:87
  340.5 56.9 %all-gather.14.cloned.1.call-done = bf16[640,1280]{0,1:T(8,128)(2,1)} async-done(((bf16[640,80]{0,1:T(8,128)(2,1)}), bf16[640,1280]{0,1:T(8,128)(2,1)}) %all-gather.14.cloned.1.call-update) | async-done | bytes 1638416 | tf_op jit(solution)/shard_map/all_gather | solution.py:88
  397.4 4.7 add_convert_fusion.5
  409.5 15.2 %all-reduce.19.cloned.1.call-done = f32[256,1280]{1,0:T(8,128)} async-done(((f32[256,1280]{1,0:T(8,128)}), f32[256,1280]{1,0:T(8,128)}) %all-reduce.19.cloned.1.call-update) | async-done | bytes 1310736 | tf_op jit(solution)/shard_map/psum | solution.py:192
  426.3 21.4 %all-reduce.17.cloned.1.call-done = bf16[256,1280]{1,0:T(8,128)(2,1)} async-done(((bf16[256,1280]{1,0:T(8,128)(2,1)}), bf16[256,1280]{1,0:T(8,128)(2,1)}) %all-reduce.17.cloned.1.call-update) | async-done | bytes 655376 | tf_op jit(solution)/shard_map/psum | solution.py:155
  451.1 58.0 %all-gather.16.cloned.1.call-done = bf16[640,1280]{0,1:T(8,128)(2,1)} async-done(((bf16[640,80]{0,1:T(8,128)(2,1)}), bf16[640,1280]{0,1:T(8,128)(2,1)}) %all-gather.16.cloned.1.call-update) | async-done | bytes 1638416 | tf_op jit(solution)/shard_map/all_gather | solution.py:167
  531.8 5.3 convolution_bitcast_fusion
  537.2 19.9 %all-reduce.21.cloned.1.call-done = f32[256,1280]{1,0:T(8,128)} async-done(((f32[256,1280]{1,0:T(8,128)}), f32[256,1280]{1,0:T(8,128)}) %all-reduce.21.cloned.1.call-update) | async-done | bytes 1310736 | tf_op jit(solution)/shard_map/psum | solution.py:231
  579.8 4.0 fusion.50
  585.0 5.5 fusion.33
  591.2 65.3 %all-reduce.8 = (f32[1280]{0:T(1024)S(1)}, f32[1280]{0:T(1024)S(1)}, f32[1280]{0:T(1024)S(1)}, f32[1280]{0:T(1024)S(1)}) all-reduce(f32[1280]{0:T(1024)S(1)} %get-tuple-element.27, f32[1280]{0:T(1024)S(1)} %get-tuple-element.25, f32[1280]{0:T(1024)S(1)} %get-tuple-element.15, ...), channel_id=3, replica_groups=mesh['fsdp'=16,'mp'=2] {'fsdp'}, use_global_device_ids=true, to_apply=%region_13.14.clone | all-reduce | flops 5120 | bytes 40960
  661.6 46.1 %reduce-scatter.24.cloned.1.call-done = f32[80,64]{1,0:T(8,128)} async-done(((f32[1280,64]{1,0:T(8,128)}), f32[80,64]{1,0:T(8,128)}) %reduce-scatter.24.cloned.1.call-update) | async-done | bytes 20496
  709.2 85.9 %reduce-scatter.18.cloned.1.call-done = f32[80,640]{1,0:T(8,128)} async-done(((f32[1280,640]{1,0:T(8,128)}), f32[80,640]{1,0:T(8,128)}) %reduce-scatter.18.cloned.1.call-update) | async-done | bytes 204816 | tf_op jit(solution)/shard_map/reduce_scatter | solution.py:258
  795.1 84.7 %reduce-scatter.20.cloned.1.call-done = f32[640,80]{0,1:T(8,128)} async-done(((f32[640,1280]{0,1:T(8,128)}), f32[640,80]{0,1:T(8,128)}) %reduce-scatter.20.cloned.1.call-update) | async-done | bytes 204816 | tf_op jit(solution)/shard_map/reduce_scatter | solution.py:259
  879.8 84.7 %reduce-scatter.16.cloned.1.call-done = f32[640,80]{0,1:T(8,128)} async-done(((f32[640,1280]{0,1:T(8,128)}), f32[640,80]{0,1:T(8,128)}) %reduce-scatter.16.cloned.1.call-update) | async-done | bytes 204816 | tf_op jit(solution)/shard_map/reduce_scatter | solution.py:256
  964.5 150.6 %reduce-scatter.12.cloned.1.call-done = f32[80,1280]{1,0:T(8,128)} async-done(((f32[1280,1280]{1,0:T(8,128)}), f32[80,1280]{1,0:T(8,128)}) %reduce-scatter.12.cloned.1.call-update) | async-done | bytes 409616 | tf_op jit(solution)/shard_map/reduce_scatter | solution.py:251
  1115.2 212.2 %reduce-scatter.14.cloned.1.call-done = f32[80,3,640]{2,0,1:T(8,128)} async-done(((f32[1280,3,640]{2,0,1:T(8,128)}), f32[80,3,640]{2,0,1:T(8,128)}) %reduce-scatter.14.cloned.1.call-update) | async-done | bytes 614416 | tf_op jit(solution)/shard_map/reduce_scatter | solution.py:255
  (273 shorter events, 138.9 us)
Async XLA Ops:
  7.2 210.1 %all-gather.8.cloned.1.call-start = ((), (), s32[]{:S(2)}) async-start(), calls=%async_computation.7 | async-start | bytes 3481600 | tf_op jit(solution)/shard_map/all_gather | solution.py:80
  7.9 213.0 %all-gather.10.cloned.1.call-start = ((), (), s32[]{:S(2)}) async-start(), calls=%async_computation.8 | async-start | bytes 5222400 | tf_op jit(solution)/shard_map/all_gather | solution.py:84
  8.7 267.6 %all-reduce.15.cloned.1.call-start = ((), (), s32[]{:S(2)}) async-start(), calls=%async_computation.9 | async-start | bytes 2621440 | tf_op jit(solution)/shard_map/psum | solution.py:149
  8.7 163.9 %collective-permute-start = (bf16[640,80]{0,1:T(8,128)(2,1)}, bf16[640,80]{0,1:T(8,128)(2,1)S(1)}, u32[]{:S(2)}, u32[]{:S(2)}) collective-permute-start(bf16[640,80]{0,1:T(8,128)(2,1)} %param.23), channel_id=1, source_target_pairs={{0,2},{2,4},{4,6},{6,8},{8,10},{10,12},{12,14},{14,16},{16,18},{18... | collective-permute-start | bytes 307208 | tf_op jit(solution)/shard_map/ppermute | solution.py:18
  10.3 162.4 %collective-permute-start.1 = (bf16[640,80]{0,1:T(8,128)(2,1)}, bf16[640,80]{0,1:T(8,128)(2,1)S(1)}, u32[]{:S(2)}, u32[]{:S(2)}) collective-permute-start(bf16[640,80]{0,1:T(8,128)(2,1)} %param.23), channel_id=1, source_target_pairs={{0,30},{2,0},{4,2},{6,4},{8,6},{10,8},{12,10},{14,12},{16,14},{18,... | collective-permute-start | bytes 307208 | tf_op jit(solution)/shard_map/ppermute | solution.py:23
  172.6 6.8 collective-permute-start.2
  172.6 6.8 collective-permute-start.3
  179.5 7.3 collective-permute-start.4
  179.5 7.3 collective-permute-start.5
  198.4 6.5 collective-permute-start.10
  198.4 6.5 collective-permute-start.11
  239.2 98.3 %all-gather.12.cloned.1.call-start = ((), (), s32[]{:S(2)}) async-start(), calls=%async_computation.10 | async-start | bytes 1740800 | tf_op jit(solution)/shard_map/all_gather | solution.py:87
  239.8 157.7 %all-gather.14.cloned.1.call-start = ((), (), s32[]{:S(2)}) async-start(), calls=%async_computation.11 | async-start | bytes 1740800 | tf_op jit(solution)/shard_map/all_gather | solution.py:88
  240.3 184.3 %all-reduce.19.cloned.1.call-start = ((), (), s32[]{:S(2)}) async-start(), calls=%async_computation.13 | async-start | bytes 2621440 | tf_op jit(solution)/shard_map/psum | solution.py:192
  404.6 43.1 %all-reduce.17.cloned.1.call-start = ((), (), s32[]{:S(2)}) async-start(), calls=%async_computation.12 | async-start | bytes 1310720 | tf_op jit(solution)/shard_map/psum | solution.py:155
  408.7 100.4 %all-gather.16.cloned.1.call-start = ((), (), s32[]{:S(2)}) async-start(), calls=%async_computation.14 | async-start | bytes 1740800 | tf_op jit(solution)/shard_map/all_gather | solution.py:167
  409.4 147.7 %all-reduce.21.cloned.1.call-start = ((), (), s32[]{:S(2)}) async-start(), calls=%async_computation.15 | async-start | bytes 2621440 | tf_op jit(solution)/shard_map/psum | solution.py:231
  537.2 123.0 %reduce-scatter.22.cloned.1.call-start = ((), (), s32[]{:S(2)}) async-start(), calls=%async_computation.21 | async-start | bytes 696320
  565.0 142.8 %reduce-scatter.24.cloned.1.call-start = ((), (), s32[]{:S(2)}) async-start(), calls=%async_computation.22 | async-start | bytes 696320
  566.3 228.8 %reduce-scatter.18.cloned.1.call-start = ((), (), s32[]{:S(2)}) async-start(), calls=%async_computation.19 | async-start | bytes 3481600 | tf_op jit(solution)/shard_map/reduce_scatter | solution.py:258
  570.1 309.8 %reduce-scatter.20.cloned.1.call-start = ((), (), s32[]{:S(2)}) async-start(), calls=%async_computation.20 | async-start | bytes 3481600 | tf_op jit(solution)/shard_map/reduce_scatter | solution.py:259
  573.7 390.8 %reduce-scatter.16.cloned.1.call-start = ((), (), s32[]{:S(2)}) async-start(), calls=%async_computation.18 | async-start | bytes 3481600 | tf_op jit(solution)/shard_map/reduce_scatter | solution.py:256
  578.5 536.7 %reduce-scatter.12.cloned.1.call-start = ((), (), s32[]{:S(2)}) async-start(), calls=%async_computation.16 | async-start | bytes 6963200 | tf_op jit(solution)/shard_map/reduce_scatter | solution.py:251
  583.8 743.5 %reduce-scatter.14.cloned.1.call-start = ((), (), s32[]{:S(2)}) async-start(), calls=%async_computation.17 | async-start | bytes 10444800 | tf_op jit(solution)/shard_map/reduce_scatter | solution.py:255
  (57 other events, 1119.8 us)
Sparse Core Ops, SparseCore 0:
  10.8 70.6 all-gather.7
  84.1 88.4 all-gather.9
  239.3 36.9 all-reduce.14
  279.2 58.2 all-gather.11
  340.4 56.9 all-gather.13
  404.7 19.8 all-reduce.18
  427.5 20.1 all-reduce.16
  450.8 58.2 all-gather.15
  537.3 19.8 all-reduce.20
  565.1 66.9 reduce-scatter.21
  634.4 73.2 reduce-scatter.23
  710.4 84.6 reduce-scatter.17
  798.0 81.8 reduce-scatter.19
  882.6 81.8 reduce-scatter.15
  967.3 147.8 reduce-scatter.11
  1118.0 209.2 reduce-scatter.13
